TPU v7x, 512 devices: a whole 4x8x8 slice. The times are simulated.
512 devices in a mesh: blk: 64 (over x, y_hi, z), head: 8 (over y_lo, core).
Axes of the slice: x: 4, y: 8 (y_hi: 2, y_lo: 4; y = y_hi * 4 + y_lo), z: 8, core: 2. Of those that a mesh axis runs over, the one named last changes fastest.
Arguments:
- query_rows: bfloat16 [16384, 2048], P('blk', 'head'), may hold values from -10 to 10
- key_rows: bfloat16 [16384, 2048], P('blk', 'head'), may hold values from -10 to 10
- value_rows: bfloat16 [16384, 2048], P('blk', 'head'), may hold values from -6 to 6
- grad_out: bfloat16 [16384, 4096], P('blk', 'head'), may hold values from -6 to 6
- out_weight: bfloat16 [2048, 4096], P('head'), may hold values from -0.09375 to 0.09375
- mask_types: int32 [128, 128], replicated, may hold values from 0 to 2, as said below
- drop_seed: int32 [1], replicated, may hold values from 0 to 1048575
Outputs:
- grad_query: bfloat16 [16384, 2048], P('blk', 'head')
- grad_key: bfloat16 [16384, 2048], P('blk', 'head')
- grad_value: bfloat16 [16384, 2048], P('blk', 'head')
Inputs may be any that keep to these rules, and one draw needn't show every extreme that they name: Blocks are runs of 128 positions. The sequence is cut into documents of whole blocks, each 1 to 4 blocks long, and some document has exactly 4 blocks. Images are pairs of blocks 2m and 2m + 1 of one document. mask_types[a, b] is 0 where blocks a and b lie in different documents; inside a document it is 2 for b < a, 2 for b = a in an image, 1 for b = a in text, 2 for b = a + 1 in one image, and 0 for other b > a. So a position sees keys only of its own shard of 256 positions and of up to 2 earlier ones.
All inputs are finite; a program needn't handle non-finite values.
Results may differ from a plain program's by a relative error of at most 0.029.
Values may be sent and summed in bfloat16 or wider, within the bound.
No kernel may reach another device: no remote copies, remote signals or barrier semaphores. Data moves between devices by JAX's collectives and lax.ppermute only.
A program may use at most 64 MiB of HBM per device.

v0:
```python
import jax
import jax.numpy as jnp
from jax import lax
from jax.sharding import PartitionSpec as P

DH = 128
HEADS_DEV = 2
MB = 128
REACH = 2
drop_level = 6554
keep_scale = 65536.0 / 58982.0
mix_one = 73244475
mix_two = 295559667
mix_three = 668265263


def shifted(value, axis, steps):
    count = lax.axis_size(axis)
    leading, last = (max(0, -steps), min(count, count - steps))
    return lax.ppermute(value, axis, [(source, source + steps) for source in range(leading, last)])


def mixhash(seed_word, head_index, query_pos, key_pos):
    hashed = query_pos * mix_one + key_pos * mix_two + head_index * mix_three + seed_word
    hashed = hashed ^ lax.shift_right_logical(hashed, jnp.int32(16))
    hashed = hashed * mix_one
    hashed = hashed ^ lax.shift_right_logical(hashed, jnp.int32(16))
    hashed = hashed * mix_one
    hashed = hashed ^ lax.shift_right_logical(hashed, jnp.int32(16))
    return (hashed & 65535 >= drop_level).astype(jnp.float32)


def visible(table_tile, query_pos, key_pos):
    return (table_tile == 2) | (table_tile == 1) & (key_pos[None, :] <= query_pos[:, None])


def expand(block_table):
    count_rows, count_cols = block_table.shape
    spread = jnp.broadcast_to(block_table[:, None, :, None], (count_rows, MB, count_cols, MB))
    return spread.reshape(count_rows * MB, count_cols * MB)


def contract_first(left, right):
    return lax.dot_general(
        left, right, (((0,), (0,)), ((), ())), preferred_element_type=jnp.float32
    )


def contract_last(left, right):
    return lax.dot_general(
        left, right, (((1,), (1,)), ((), ())), preferred_element_type=jnp.float32
    )


def on_device(query_rows, key_rows, value_rows, grad_out, out_weight, mask_types, drop_seed):
    row_count = query_rows.shape[0]
    span_rows = (REACH + 1) * row_count
    block_rows = row_count // MB
    margin_blocks = REACH * block_rows
    span_blocks = span_rows // MB
    score_scale = DH ** (-0.5)
    seed_word = drop_seed[0]
    device = lax.axis_index("blk")
    head_base = lax.axis_index("head") * HEADS_DEV
    own_pos = device * row_count + jnp.arange(row_count, dtype=jnp.int32)
    window_pos = (device - REACH) * row_count + jnp.arange(span_rows, dtype=jnp.int32)
    padded_table = jnp.pad(mask_types, margin_blocks)
    near_table = lax.dynamic_slice(
        padded_table,
        (device * block_rows + margin_blocks, device * block_rows),
        (block_rows, span_blocks),
    )
    allowed = visible(expand(near_table), own_pos, window_pos)
    grad_attn = contract_last(
        lax.all_gather(grad_out, "head", axis=1, tiled=True), out_weight
    ).astype(jnp.bfloat16)
    offsets = [distance for distance in range(1, REACH + 1)]
    stacked = jnp.stack((key_rows, value_rows))
    key_slots = [stacked for slot_index in range(REACH + 1)]
    for distance in offsets:
        key_slots[REACH - distance] = shifted(stacked, "blk", distance)
    windowed = jnp.concatenate(key_slots, axis=1)
    query_grads = []
    key_parts = []
    value_parts = []
    total_cols = []
    dot_cols = []
    for local_head in range(HEADS_DEV):
        head_index = head_base + local_head
        first_col = local_head * DH
        last_col = first_col + DH
        query_head = query_rows[:, first_col:last_col]
        grad_head = grad_attn[:, first_col:last_col]
        key_window = windowed[0, :, first_col:last_col]
        value_window = windowed[1, :, first_col:last_col]
        scores = contract_last(query_head, key_window) * score_scale
        masked = jnp.where(allowed, scores, -jnp.inf)
        row_max = jnp.max(masked, axis=1, keepdims=True)
        log_total = row_max + jnp.log(jnp.sum(jnp.exp(masked - row_max), axis=1, keepdims=True))
        attn_prob = jnp.where(allowed, jnp.exp(scores - log_total), 0.0)
        keep_mask = (
            mixhash(seed_word, head_index, own_pos[:, None], window_pos[None, :]) * keep_scale
        )
        dropped = (attn_prob * keep_mask).astype(jnp.bfloat16)
        attended = jnp.dot(dropped, value_window, preferred_element_type=jnp.float32).astype(
            jnp.bfloat16
        )
        row_dot = jnp.sum(
            grad_head.astype(jnp.float32) * attended.astype(jnp.float32), axis=1, keepdims=True
        )
        grad_prob = contract_last(grad_head, value_window)
        dscore = (attn_prob * (grad_prob * keep_mask - row_dot)).astype(jnp.bfloat16)
        query_grads.append(
            jnp.dot(dscore, key_window, preferred_element_type=jnp.float32) * score_scale
        )
        total_cols.append(log_total)
        dot_cols.append(row_dot)
        key_parts.append(contract_first(dscore, query_head) * score_scale)
        value_parts.append(contract_first(dropped, grad_head))
    grad_query = jnp.concatenate(query_grads, axis=1).astype(jnp.bfloat16)
    partials = jnp.stack((jnp.concatenate(key_parts, axis=1), jnp.concatenate(value_parts, axis=1)))
    summed = partials[:, REACH * row_count : (REACH + 1) * row_count]
    for distance in offsets:
        slot_index = REACH - distance
        outgoing = partials[:, slot_index * row_count : (slot_index + 1) * row_count]
        summed = summed + shifted(outgoing, "blk", -distance)
    grad_key = summed[0].astype(jnp.bfloat16)
    grad_value = summed[1].astype(jnp.bfloat16)
    return (grad_query, grad_key, grad_value)


def solution(mesh):
    in_specs = (
        P("blk", "head"),
        P("blk", "head"),
        P("blk", "head"),
        P("blk", "head"),
        P("head", None),
        P(),
        P(),
    )
    out_specs = (P("blk", "head"), P("blk", "head"), P("blk", "head"))
    return jax.shard_map(
        on_device, mesh=mesh, in_specs=in_specs, out_specs=out_specs, check_vma=False
    )
```

profile of v0, /device:TPU:6, one launch (start us, length us, event | category | flops | bytes accessed | tf_op | source)
XLA Modules:
  0.0 147.7 jit_solution(5357728235868405602)
XLA Ops:
  7.2 0.0 copy-start
  7.2 0.0 all-gather.2.cloned.1.call-start
  7.2 0.7 all-gather.2.cloned.1.call-update
  7.9 1.0 pad_maximum_fusion.1
  8.9 4.3 %collective-permute-start.1 = (bf16[2,256,256]{2,1,0:T(8,128)(2,1)S(1)}, bf16[2,256,256]{2,1,0:T(8,128)(2,1)S(1)}, u32[]{:S(2)}, u32[]{:S(2)}) collective-permute-start(bf16[2,256,256]{2,1,0:T(8,128)(2,1)S(1)} %pad_maximum_fusion.1), channel_id=1, source_target_pairs={{0,8},{8,16},{16,24},{24,32},{32,40},{40,48},{48,56},{56,64},{64,7... | collective-permute-start | bytes 786440 | tf_op jit(solution)/shard_map/ppermute | solution.py:20
  13.2 6.1 %collective-permute-start = (bf16[2,256,256]{2,1,0:T(8,128)(2,1)S(1)}, bf16[2,256,256]{2,1,0:T(8,128)(2,1)S(1)}, u32[]{:S(2)}, u32[]{:S(2)}) collective-permute-start(bf16[2,256,256]{2,1,0:T(8,128)(2,1)S(1)} %pad_maximum_fusion.1), channel_id=1, source_target_pairs={{0,16},{8,24},{16,32},{24,40},{32,48},{40,56},{48,64},{56,72},{64,... | collective-permute-start | bytes 786440 | tf_op jit(solution)/shard_map/ppermute | solution.py:20
  19.3 0.8 broadcast_compare_fusion
  20.8 0.1 broadcast_in_dim.13
  20.9 0.1 copy.31
  21.1 0.0 copy-start.8
  21.1 0.3 copy.18
  21.4 0.1 broadcast_in_dim.14
  21.5 0.1 copy.30
  21.6 1.0 copy.17
  22.6 13.1 %collective-permute-done.1 = bf16[2,256,256]{2,1,0:T(8,128)(2,1)S(1)} collective-permute-done((bf16[2,256,256]{2,1,0:T(8,128)(2,1)S(1)}, bf16[2,256,256]{2,1,0:T(8,128)(2,1)S(1)}, u32[]{:S(2)}, u32[]{:S(2)}) %collective-permute-start.1) | collective-permute-done | bytes 262176 | tf_op jit(solution)/shard_map/ppermute | solution.py:20
  35.7 5.8 %collective-permute-done = bf16[2,256,256]{2,1,0:T(8,128)(2,1)S(1)} collective-permute-done((bf16[2,256,256]{2,1,0:T(8,128)(2,1)S(1)}, bf16[2,256,256]{2,1,0:T(8,128)(2,1)S(1)}, u32[]{:S(2)}, u32[]{:S(2)}) %collective-permute-start) | collective-permute-done | bytes 262176 | tf_op jit(solution)/shard_map/ppermute | solution.py:20
  41.5 0.0 copy-done.6
  41.5 0.1 maximum_maximum_fusion
  41.6 0.0 copy-done.8
  41.6 0.0 copy-start.2
  41.6 0.3 fusion.4
  41.9 0.5 fusion.33
  42.4 0.1 copy-done.2
  42.5 0.9 copy-done.4
  43.4 0.3 exponential_reduce_fusion.1
  43.7 12.8 %all-gather.2.cloned.1.call-done = bf16[256,4096]{1,0:T(8,128)(2,1)} async-done(((bf16[256,512]{1,0:T(8,128)(2,1)}), bf16[256,4096]{1,0:T(8,128)(2,1)}) %all-gather.2.cloned.1.call-update) | async-done | bytes 2097168 | tf_op jit(solution)/shard_map/all_gather | solution.py:75
  56.6 2.4 %convolution_convert_fusion = bf16[256,256]{0,1:T(8,128)(2,1)S(1)} fusion(bf16[256,4096]{1,0:T(8,128)(2,1)} %all-gather.2.cloned.1.call-done, bf16[256,4096]{1,0:T(8,128)(2,1)S(1)} %copy-done), kind=kOutput, calls=%fused_computation.24 | convolution fusion | flops 536936448 | bytes 4325376 | tf_op jit(solution)/shard_map/dot_general | solution.py:50
  59.0 0.8 fusion.15
  59.9 0.8 fusion.42
  60.6 0.7 fusion.6
  61.4 0.3 convolution_multiply_fusion.5
  61.6 0.8 fusion.14
  62.5 0.8 fusion.39
  63.2 0.7 fusion.7
  64.0 0.3 convolution_multiply_fusion.4
  64.2 0.1 maximum_bitcast_fusion.1
  64.3 0.1 maximum_bitcast_fusion
  64.4 1.0 fusion.28
  65.4 18.8 %collective-permute-start.2 = (f32[2,256,256]{1,2,0:T(8,128)}, f32[2,256,256]{1,2,0:T(8,128)}, u32[]{:S(2)}, u32[]{:S(2)}) collective-permute-start(f32[2,256,256]{1,2,0:T(8,128)} %get-tuple-element.16), channel_id=1, source_target_pairs={{8,0},{16,8},{24,16},{32,24},{40,32},{48,40},{56,48},{64,56},{72,6... | collective-permute-start | bytes 1572872 | tf_op jit(solution)/shard_map/ppermute | solution.py:20
  84.2 1.9 %collective-permute-start.3 = (f32[2,256,256]{1,2,0:T(8,128)S(1)}, f32[2,256,256]{1,2,0:T(8,128)}, u32[]{:S(2)}, u32[]{:S(2)}) collective-permute-start(f32[2,256,256]{1,2,0:T(8,128)S(1)} %get-tuple-element.17), channel_id=1, source_target_pairs={{16,0},{24,8},{32,16},{40,24},{48,32},{56,40},{64,48},{72,56},{80,... | collective-permute-start | bytes 1572872 | tf_op jit(solution)/shard_map/ppermute | solution.py:20
  86.2 0.3 fusion.8
  86.5 0.3 fusion.9
  86.7 0.8 copy.21
  87.5 40.2 %collective-permute-done.2 = f32[2,256,256]{1,2,0:T(8,128)} collective-permute-done((f32[2,256,256]{1,2,0:T(8,128)}, f32[2,256,256]{1,2,0:T(8,128)}, u32[]{:S(2)}, u32[]{:S(2)}) %collective-permute-start.2) | collective-permute-done | bytes 524320 | tf_op jit(solution)/shard_map/ppermute | solution.py:20
  127.7 10.3 %collective-permute-done.3 = f32[2,256,256]{1,2,0:T(8,128)} collective-permute-done((f32[2,256,256]{1,2,0:T(8,128)S(1)}, f32[2,256,256]{1,2,0:T(8,128)}, u32[]{:S(2)}, u32[]{:S(2)}) %collective-permute-start.3) | collective-permute-done | bytes 524320 | tf_op jit(solution)/shard_map/ppermute | solution.py:20
  138.0 1.3 fusion.32
  139.3 0.8 copy.23
  140.1 0.8 copy.22
  (21 shorter events, 0.1 us)
Async XLA Ops:
  7.2 49.4 %copy-start = (bf16[256,4096]{1,0:T(8,128)(2,1)S(1)}, bf16[256,4096]{1,0:T(8,128)(2,1)}, u32[]{:S(2)}) copy-start(bf16[256,4096]{1,0:T(8,128)(2,1)} %param.11) | copy-start | bytes 6291460
  7.2 34.4 %copy-start.6 = (bf16[256,256]{1,0:T(8,128)(2,1)S(1)}, bf16[256,256]{1,0:T(8,128)(2,1)}, u32[]{:S(2)}) copy-start(bf16[256,256]{1,0:T(8,128)(2,1)} %param.9) | copy-start | bytes 393220
  7.2 34.4 %copy-start.7 = (bf16[256,256]{1,0:T(8,128)(2,1)S(1)}, bf16[256,256]{1,0:T(8,128)(2,1)}, u32[]{:S(2)}) copy-start(bf16[256,256]{1,0:T(8,128)(2,1)} %param.8) | copy-start | bytes 393220
  7.2 49.4 %all-gather.2.cloned.1.call-start = ((), (), s32[]{:S(2)}) async-start(), calls=%async_computation | async-start | bytes 2359296 | tf_op jit(solution)/shard_map/all_gather | solution.py:75
  8.9 26.8 %collective-permute-start.1 = (bf16[2,256,256]{2,1,0:T(8,128)(2,1)S(1)}, bf16[2,256,256]{2,1,0:T(8,128)(2,1)S(1)}, u32[]{:S(2)}, u32[]{:S(2)}) collective-permute-start(bf16[2,256,256]{2,1,0:T(8,128)(2,1)S(1)} %pad_maximum_fusion.1), channel_id=1, source_target_pairs={{0,8},{8,16},{16,24},{24,32},{32,40},{40,48},{48,56},{56,64},{64,7... | collective-permute-start | bytes 786440 | tf_op jit(solution)/shard_map/ppermute | solution.py:20
  13.2 28.3 %collective-permute-start = (bf16[2,256,256]{2,1,0:T(8,128)(2,1)S(1)}, bf16[2,256,256]{2,1,0:T(8,128)(2,1)S(1)}, u32[]{:S(2)}, u32[]{:S(2)}) collective-permute-start(bf16[2,256,256]{2,1,0:T(8,128)(2,1)S(1)} %pad_maximum_fusion.1), channel_id=1, source_target_pairs={{0,16},{8,24},{16,32},{24,40},{32,48},{40,56},{48,64},{56,72},{64,... | collective-permute-start | bytes 786440 | tf_op jit(solution)/shard_map/ppermute | solution.py:20
  21.1 20.6 %copy-start.8 = (bf16[256,256]{1,0:T(8,128)(2,1)S(1)}, bf16[256,256]{1,0:T(8,128)(2,1)}, u32[]{:S(2)}) copy-start(bf16[256,256]{1,0:T(8,128)(2,1)} %param.7) | copy-start | bytes 393220
  22.6 19.3 %copy-start.9 = (pred[256,768]{0,1:T(32,128)(4,1)S(1)}, pred[256,768]{0,1:T(32,128)(4,1)}, u32[]{:S(2)}) copy-start(pred[256,768]{0,1:T(32,128)(4,1)} %copy.17) | copy-start | bytes 589828
  41.6 0.9 copy-start.2
  42.5 0.9 copy-start.4
  56.6 2.5 %copy-start.3 = (bf16[2,768,256]{2,1,0:T(8,128)(2,1)S(1)}, bf16[2,768,256]{2,1,0:T(8,128)(2,1)}, u32[]{:S(2)}) copy-start(bf16[2,768,256]{2,1,0:T(8,128)(2,1)} %copy-done.2) | copy-start | bytes 2359300
  56.6 2.5 %copy-start.5 = (f32[256,768]{0,1:T(8,128)S(1)}, f32[256,768]{0,1:T(8,128)}, u32[]{:S(2)}) copy-start(f32[256,768]{0,1:T(8,128)} %copy-done.4) | copy-start | bytes 2359300
  64.4 22.1 %copy-start.1 = (f32[1,768,256]{1,2,0:T(8,128)}, f32[1,768,256]{1,2,0:T(8,128)S(1)}, u32[]{:S(2)}) copy-start(f32[1,768,256]{1,2,0:T(8,128)S(1)} %maximum_bitcast_fusion) | copy-start | bytes 2359300
  65.4 62.3 %collective-permute-start.2 = (f32[2,256,256]{1,2,0:T(8,128)}, f32[2,256,256]{1,2,0:T(8,128)}, u32[]{:S(2)}, u32[]{:S(2)}) collective-permute-start(f32[2,256,256]{1,2,0:T(8,128)} %get-tuple-element.16), channel_id=1, source_target_pairs={{8,0},{16,8},{24,16},{32,24},{40,32},{48,40},{56,48},{64,56},{72,6... | collective-permute-start | bytes 1572872 | tf_op jit(solution)/shard_map/ppermute | solution.py:20
  84.2 53.7 %collective-permute-start.3 = (f32[2,256,256]{1,2,0:T(8,128)S(1)}, f32[2,256,256]{1,2,0:T(8,128)}, u32[]{:S(2)}, u32[]{:S(2)}) collective-permute-start(f32[2,256,256]{1,2,0:T(8,128)S(1)} %get-tuple-element.17), channel_id=1, source_target_pairs={{16,0},{24,8},{32,16},{40,24},{48,32},{56,40},{64,48},{72,56},{80,... | collective-permute-start | bytes 1572872 | tf_op jit(solution)/shard_map/ppermute | solution.py:20
Sparse Core Ops, SparseCore 0:
  10.1 46.3 all-gather.1
where the time goes:
time: 148 us
  waiting for transfers between devices  82.9 us (56%)
  starting transfers between devices  31.2 us (21%)
  between operations  15 us (10%)
  matrix products  8.92 us (6%)
  local copies, waits for them, and re-layouts  5.06 us (3%)
  other arithmetic  4.67 us (3%)
    ppermute x4, waiting for transfers between devices, shifted(): lax.ppermute(value, axis, [(source, source + steps) for source in range(l...  69.4 us
    ppermute x4, starting transfers between devices, shifted(): lax.ppermute(value, axis, [(source, source + steps) for source in range(l...  31.1 us
    all_gather x1, waiting for transfers between devices, on_device(): lax.all_gather(grad_out, 'head', axis=1, tiled=True)  12.8 us
    dot_general x5, matrix products, contract_last(): lax.dot_general(left, right, (((1,), (1,)), ((), ())), preferred_element_...  4.61 us
    unnamed x25, local copies, waits for them, and re-layouts  3.5 us
  transfers between devices with their start and end apart: 5, of which 5 were waited for; matrix products, arithmetic and copies ran while one was open for 4% of the time, Pallas kernels for 0%

commit v1 on v0

--- a/solution.py
+++ b/solution.py
@@ -72,7 +72,10 @@
     )
     allowed = visible(expand(near_table), own_pos, window_pos)
     grad_attn = contract_last(
-        lax.all_gather(grad_out, "head", axis=1, tiled=True), out_weight
+        jnp.concatenate(
+            lax.all_to_all(jnp.stack([grad_out] * lax.axis_size("head")), "head", 0, 0), axis=1
+        ),
+        out_weight,
     ).astype(jnp.bfloat16)
     offsets = [distance for distance in range(1, REACH + 1)]
     stacked = jnp.stack((key_rows, value_rows))

time: 148 us -> 153 us (1.034)
  the two profiles are of different devices: /device:TPU:6 before, /device:TPU:2 now
where the time goes in v1:
time: 153 us; the launch traced here: 152 us
  waiting for transfers between devices  95.1 us (62%)
  starting transfers between devices  35.7 us (23%)
  matrix products  8.81 us (6%)
  local copies, waits for them, and re-layouts  7.87 us (5%)
  other arithmetic  3.01 us (2%)
  between operations  1.63 us (1%)
    ppermute x4, waiting for transfers between devices, shifted(): lax.ppermute(value, axis, [(source, source + steps) for source in range(l...  95.1 us
    ppermute x4, starting transfers between devices, shifted(): lax.ppermute(value, axis, [(source, source + steps) for source in range(l...  30.7 us
    all_to_all x1, starting transfers between devices, on_device(): lax.all_to_all(jnp.stack([grad_out] * lax.axis_size('head')), 'head', 0, 0)  5.01 us
    unnamed x28, local copies, waits for them, and re-layouts  4.9 us
    dot_general x5, matrix products, contract_last(): lax.dot_general(left, right, (((1,), (1,)), ((), ())), preferred_element_...  4.5 us
  transfers between devices with their start and end apart: 5, of which 3 were waited for; matrix products, arithmetic and copies ran while one was open for 3% of the time, Pallas kernels for 0%

profile of v1, /device:TPU:2, one launch (start us, length us, event | category | flops | bytes accessed | tf_op | source)
XLA Modules:
  0.0 152.1 jit_solution(4348371017736450569)
XLA Ops:
  0.6 0.0 copy-start
  0.6 1.2 copy.19
  1.9 1.4 stack.32
  3.3 5.0 %all-to-all-start = ((bf16[8,256,512]{1,2,0:T(8,128)(2,1)}), bf16[8,256,512]{1,2,0:T(8,128)(2,1)}, u32[]{:S(2)}, u32[]{:S(2)}) async-start(bf16[8,256,512]{1,2,0:T(8,128)(2,1)} %stack.32), calls=%async_computation | async-start | bytes 4194304 | tf_op jit(solution)/shard_map/all_to_all | solution.py:76
  8.3 0.0 copy-done.6
  8.4 4.3 %collective-permute-start.1 = (bf16[2,256,256]{2,1,0:T(8,128)(2,1)S(1)}, bf16[2,256,256]{2,1,0:T(8,128)(2,1)S(1)}, u32[]{:S(2)}, u32[]{:S(2)}) collective-permute-start(bf16[2,256,256]{2,1,0:T(8,128)(2,1)S(1)} %pad_maximum_fusion.1), channel_id=1, source_target_pairs={{0,8},{8,16},{16,24},{24,32},{32,40},{40,48},{48,56},{56,64},{64,7... | collective-permute-start | bytes 786440 | tf_op jit(solution)/shard_map/ppermute | solution.py:20
  12.7 6.1 %collective-permute-start = (bf16[2,256,256]{2,1,0:T(8,128)(2,1)S(1)}, bf16[2,256,256]{2,1,0:T(8,128)(2,1)S(1)}, u32[]{:S(2)}, u32[]{:S(2)}) collective-permute-start(bf16[2,256,256]{2,1,0:T(8,128)(2,1)S(1)} %pad_maximum_fusion.1), channel_id=1, source_target_pairs={{0,16},{8,24},{16,32},{24,40},{32,48},{40,56},{48,64},{56,72},{64,... | collective-permute-start | bytes 786440 | tf_op jit(solution)/shard_map/ppermute | solution.py:20
  18.8 0.1 broadcast_compare_fusion
  18.9 0.1 broadcast_in_dim.13
  19.0 0.1 copy.32
  19.2 0.0 copy-start.8
  19.2 0.3 copy.18
  19.5 0.1 broadcast_in_dim.14
  19.6 0.1 copy.31
  19.7 1.0 copy.17
  21.4 53.5 %collective-permute-done.1 = bf16[2,256,256]{2,1,0:T(8,128)(2,1)S(1)} collective-permute-done((bf16[2,256,256]{2,1,0:T(8,128)(2,1)S(1)}, bf16[2,256,256]{2,1,0:T(8,128)(2,1)S(1)}, u32[]{:S(2)}, u32[]{:S(2)}) %collective-permute-start.1) | collective-permute-done | bytes 262176 | tf_op jit(solution)/shard_map/ppermute | solution.py:20
  74.9 0.0 collective-permute-done
  74.9 0.1 maximum_maximum_fusion
  75.0 0.3 fusion.4
  75.2 0.5 fusion.33
  75.7 0.1 copy-done.2
  75.8 0.9 copy-done.4
  76.7 0.3 exponential_reduce_fusion.1
  77.1 0.0 all-to-all-done
  77.1 2.4 %convolution_convert_fusion = bf16[256,256]{0,1:T(8,128)(2,1)S(1)} fusion(bf16[256,4096]{1,0:T(8,128)(2,1)S(1)} %copy-done, bf16[256,4096]{0,1:T(8,128)(2,1)} %bitcast.5), kind=kOutput, calls=%fused_computation.24 | convolution fusion | flops 536936448 | bytes 4325376 | tf_op jit(solution)/shard_map/dot_general | solution.py:50
  79.5 0.8 fusion.14
  80.3 0.0 copy-start.5
  80.3 0.7 fusion.7
  81.0 0.3 convolution_multiply_fusion.4
  81.3 0.1 copy-done.5
  81.5 0.8 fusion.15
  82.3 0.7 fusion.6
  83.0 0.3 convolution_multiply_fusion.5
  83.3 0.8 fusion.39
  84.0 0.8 fusion.42
  84.8 0.1 maximum_bitcast_fusion
  84.9 0.1 maximum_bitcast_fusion.1
  85.0 1.0 fusion.28
  86.0 7.2 %collective-permute-start.3 = (f32[2,256,256]{1,2,0:T(8,128)}, f32[2,256,256]{1,2,0:T(8,128)}, u32[]{:S(2)}, u32[]{:S(2)}) collective-permute-start(f32[2,256,256]{1,2,0:T(8,128)} %get-tuple-element.17), channel_id=1, source_target_pairs={{16,0},{24,8},{32,16},{40,24},{48,32},{56,40},{64,48},{72,56},{80,... | collective-permute-start | bytes 1572872 | tf_op jit(solution)/shard_map/ppermute | solution.py:20
  93.2 13.2 %collective-permute-start.2 = (f32[2,256,256]{1,2,0:T(8,128)S(1)}, f32[2,256,256]{1,2,0:T(8,128)}, u32[]{:S(2)}, u32[]{:S(2)}) collective-permute-start(f32[2,256,256]{1,2,0:T(8,128)S(1)} %get-tuple-element.16), channel_id=1, source_target_pairs={{8,0},{16,8},{24,16},{32,24},{40,32},{48,40},{56,48},{64,56},{72,6... | collective-permute-start | bytes 1572872 | tf_op jit(solution)/shard_map/ppermute | solution.py:20
  106.3 0.3 fusion.9
  106.6 0.3 fusion.8
  106.9 0.8 copy.22
  107.7 28.6 %collective-permute-done.3 = f32[2,256,256]{1,2,0:T(8,128)} collective-permute-done((f32[2,256,256]{1,2,0:T(8,128)}, f32[2,256,256]{1,2,0:T(8,128)}, u32[]{:S(2)}, u32[]{:S(2)}) %collective-permute-start.3) | collective-permute-done | bytes 524320 | tf_op jit(solution)/shard_map/ppermute | solution.py:20
  136.3 12.9 %collective-permute-done.2 = f32[2,256,256]{1,2,0:T(8,128)} collective-permute-done((f32[2,256,256]{1,2,0:T(8,128)S(1)}, f32[2,256,256]{1,2,0:T(8,128)}, u32[]{:S(2)}, u32[]{:S(2)}) %collective-permute-start.2) | collective-permute-done | bytes 524320 | tf_op jit(solution)/shard_map/ppermute | solution.py:20
  149.2 1.3 fusion.32
  150.6 0.8 copy.23
  151.4 0.8 copy.24
  (24 shorter events, 0.1 us)
Async XLA Ops:
  0.6 76.5 %copy-start = (bf16[256,4096]{1,0:T(8,128)(2,1)S(1)}, bf16[256,4096]{1,0:T(8,128)(2,1)}, u32[]{:S(2)}) copy-start(bf16[256,4096]{1,0:T(8,128)(2,1)} %param.11) | copy-start | bytes 6291460
  3.3 5.0 %copy-start.6 = (bf16[256,256]{1,0:T(8,128)(2,1)S(1)}, bf16[256,256]{1,0:T(8,128)(2,1)}, u32[]{:S(2)}) copy-start(bf16[256,256]{1,0:T(8,128)(2,1)} %param.9) | copy-start | bytes 393220
  3.3 5.0 %copy-start.7 = (bf16[256,256]{1,0:T(8,128)(2,1)S(1)}, bf16[256,256]{1,0:T(8,128)(2,1)}, u32[]{:S(2)}) copy-start(bf16[256,256]{1,0:T(8,128)(2,1)} %param.8) | copy-start | bytes 393220
  3.3 15.5 %copy-start.10 = (s32[128,128]{1,0:T(8,128)S(1)}, s32[128,128]{1,0:T(8,128)}, u32[]{:S(2)}) copy-start(s32[128,128]{1,0:T(8,128)} %param.12) | copy-start | bytes 196612
  3.3 73.8 %all-to-all-start = ((bf16[8,256,512]{1,2,0:T(8,128)(2,1)}), bf16[8,256,512]{1,2,0:T(8,128)(2,1)}, u32[]{:S(2)}, u32[]{:S(2)}) async-start(bf16[8,256,512]{1,2,0:T(8,128)(2,1)} %stack.32), calls=%async_computation | async-start | bytes 4194304 | tf_op jit(solution)/shard_map/all_to_all | solution.py:76
  8.4 66.5 %collective-permute-start.1 = (bf16[2,256,256]{2,1,0:T(8,128)(2,1)S(1)}, bf16[2,256,256]{2,1,0:T(8,128)(2,1)S(1)}, u32[]{:S(2)}, u32[]{:S(2)}) collective-permute-start(bf16[2,256,256]{2,1,0:T(8,128)(2,1)S(1)} %pad_maximum_fusion.1), channel_id=1, source_target_pairs={{0,8},{8,16},{16,24},{24,32},{32,40},{40,48},{48,56},{56,64},{64,7... | collective-permute-start | bytes 786440 | tf_op jit(solution)/shard_map/ppermute | solution.py:20
  12.7 62.2 %collective-permute-start = (bf16[2,256,256]{2,1,0:T(8,128)(2,1)S(1)}, bf16[2,256,256]{2,1,0:T(8,128)(2,1)S(1)}, u32[]{:S(2)}, u32[]{:S(2)}) collective-permute-start(bf16[2,256,256]{2,1,0:T(8,128)(2,1)S(1)} %pad_maximum_fusion.1), channel_id=1, source_target_pairs={{0,16},{8,24},{16,32},{24,40},{32,48},{40,56},{48,64},{56,72},{64,... | collective-permute-start | bytes 786440 | tf_op jit(solution)/shard_map/ppermute | solution.py:20
  19.2 55.8 %copy-start.8 = (bf16[256,256]{1,0:T(8,128)(2,1)S(1)}, bf16[256,256]{1,0:T(8,128)(2,1)}, u32[]{:S(2)}) copy-start(bf16[256,256]{1,0:T(8,128)(2,1)} %param.7) | copy-start | bytes 393220
  21.3 53.9 %copy-start.9 = (pred[256,768]{0,1:T(32,128)(4,1)S(1)}, pred[256,768]{0,1:T(32,128)(4,1)}, u32[]{:S(2)}) copy-start(pred[256,768]{0,1:T(32,128)(4,1)} %copy.17) | copy-start | bytes 589828
  74.9 0.9 copy-start.2
  75.8 0.9 copy-start.4
  77.1 2.4 %copy-start.3 = (bf16[2,768,256]{2,1,0:T(8,128)(2,1)S(1)}, bf16[2,768,256]{2,1,0:T(8,128)(2,1)}, u32[]{:S(2)}) copy-start(bf16[2,768,256]{2,1,0:T(8,128)(2,1)} %copy-done.2) | copy-start | bytes 2359300
  80.3 1.1 copy-start.5
  84.9 21.7 %copy-start.1 = (f32[1,768,256]{1,2,0:T(8,128)}, f32[1,768,256]{1,2,0:T(8,128)S(1)}, u32[]{:S(2)}) copy-start(f32[1,768,256]{1,2,0:T(8,128)S(1)} %maximum_bitcast_fusion.1) | copy-start | bytes 2359300
  86.0 50.3 %collective-permute-start.3 = (f32[2,256,256]{1,2,0:T(8,128)}, f32[2,256,256]{1,2,0:T(8,128)}, u32[]{:S(2)}, u32[]{:S(2)}) collective-permute-start(f32[2,256,256]{1,2,0:T(8,128)} %get-tuple-element.17), channel_id=1, source_target_pairs={{16,0},{24,8},{32,16},{40,24},{48,32},{56,40},{64,48},{72,56},{80,... | collective-permute-start | bytes 1572872 | tf_op jit(solution)/shard_map/ppermute | solution.py:20
  93.2 56.1 %collective-permute-start.2 = (f32[2,256,256]{1,2,0:T(8,128)S(1)}, f32[2,256,256]{1,2,0:T(8,128)}, u32[]{:S(2)}, u32[]{:S(2)}) collective-permute-start(f32[2,256,256]{1,2,0:T(8,128)S(1)} %get-tuple-element.16), channel_id=1, source_target_pairs={{8,0},{16,8},{24,16},{32,24},{40,32},{48,40},{56,48},{64,56},{72,6... | collective-permute-start | bytes 1572872 | tf_op jit(solution)/shard_map/ppermute | solution.py:20
